TPU v7x, 256 devices: a whole 4x4x8 slice. The times are simulated.
256 devices in a mesh: rep: 32 (over z, y_lo, core), tp: 8 (over x, y_hi).
Axes of the slice: x: 4, y: 4 (y_hi: 2, y_lo: 2; y = y_hi * 2 + y_lo), z: 8, core: 2. Of those that a mesh axis runs over, the one named last changes fastest.
Arguments:
- context: bfloat16 [8192, 3072], P('rep', 'tp'), may hold values from -6 to 6
- residual: bfloat16 [8192, 5120], P(('rep', 'tp')), may hold values from -6 to 6
- cotangent: bfloat16 [8192, 5120], P(('rep', 'tp')), may hold values from -6 to 6
- numer: bfloat16 [32, 3072, 5120], P('rep', 'tp'), may hold values from -0.109375 to 0.109375
- weight: float32 [32], P('rep'), may hold values from 0.5 to 2
- step: int32 [1], replicated, may hold values from 0 to 999999
Outputs:
- output: bfloat16 [8192, 5120], P(('rep', 'tp'))
- grad_context: bfloat16 [8192, 3072], P('rep', 'tp')
- numer_next: bfloat16 [32, 3072, 5120], P('rep', 'tp')
- weight_next: float32 [32], P('rep')
All inputs are finite; a program needn't handle non-finite values.
Results may differ from a plain program's by a relative error of at most 0.013.
Values may be sent and summed in bfloat16 or wider, within the bound.
A program may use at most 192 MiB of HBM per device.

v0:
```python
import functools

import jax
import jax.numpy as jnp
from jax import lax
from jax.experimental import pallas as pl
from jax.experimental.pallas import tpu as pltpu
from jax.sharding import PartitionSpec as P

PEER_BITS = 3
LEARN = 0.001
MESH = pl.DeviceIdType.MESH
WIDE = 256
FLAT = 1024

PLANS = (
    (((1,), 32, 12),),
    (((2,), 32, 12),),
    (((-12, -12, -4), 16, 2), ((4,), 32, 11)),
    (((-12, -12), 16, 6), ((8,), 32, 9)),
)
EARLY = (5, 5, 13, 15)


def pieces_of(k):
    row, pieces = 0, []
    for legs, rows, count in PLANS[k]:
        for _ in range(count):
            pieces.append((row, rows, legs))
            row += rows
    return row, pieces


def kernel(k, reps, tps, names, *refs):
    r = dict(zip(names, refs, strict=True))
    rep, tp = lax.axis_index("rep"), lax.axis_index("tp")
    x, y_hi = tp // 2, tp % 2
    over = rep + 2 - 4 * ((rep // 2) % 2)
    flip = tp + 1 - 2 * y_hi
    ahead, behind = (tp + 2) % tps, (tp + tps - 2) % tps
    at = lambda a, b: {"rep": a, "tp": b}
    _, pieces = pieces_of(k)
    feats, wide = r["numer"].shape
    toks = r["cot"].shape[0]

    used = {"s": 0, "r": 0}
    sends = []

    def send(src, dst, where):
        i = used["s"]
        used["s"] += 1
        copy = pltpu.make_async_remote_copy(
            src_ref=src,
            dst_ref=dst,
            send_sem=r["ss"].at[i],
            recv_sem=r["rs"].at[i],
            device_id=where,
            device_id_type=MESH,
        )
        copy.start()
        sends.append(copy)
        return copy

    def local(src, dst):
        i = used["r"]
        used["r"] += 1
        copy = pltpu.make_async_copy(src, dst, r["ls"].at[i])
        copy.start()
        return copy

    def tiles(n, body):
        def step(j, carry):
            body(pl.ds(pl.multiple_of(j * n, n), n))
            return carry

        lax.fori_loop(0, wide // n, step, 0)

    f32 = lambda a: a.astype(jnp.float32)
    bf16 = lambda a: a.astype(jnp.bfloat16)

    loads = [
        local(r["numer"], r["numer_v"]),
        local(r["ctx"], r["ctx_v"]),
        local(r["cot"], r["cots"].at[tp]),
        local(r["res"], r["res_v"]),
    ]
    weight = r["weight"][0]
    r["w_out"][...] = jnp.full(r["w_out"].shape, weight, jnp.float32)

    hops = sorted({hop for _, _, legs in pieces for hop in legs} | {1 << k})
    near = [at(over, tp), at(over, flip), at(rep, ahead), at(rep, behind)]
    near += [at((rep + sign * hop) % reps, tp) for hop in hops for sign in (1, -1)]
    barrier = pltpu.get_barrier_semaphore()
    for where in near:
        pl.semaphore_signal(barrier, inc=1, device_id=where, device_id_type=MESH)
    pl.semaphore_wait(barrier, len(near))

    a1 = send(r["cot"], r["y_relay"].at[0], at(over, tp))
    b_up = send(r["cot"], r["cots"].at[tp], at(rep, ahead))
    b_down = send(r["cot"], r["cots"].at[tp], at(rep, behind))

    arrived = {}

    def leg(p, i):
        row, rows, legs = pieces[p]
        where = at((rep + legs[i]) % reps, tp)
        span = pl.ds(row, rows)
        src = r["numer"].at[span] if i == 0 else r["legs"].at[i - 1, span]
        dst = r["peer_v"].at[span] if i == len(legs) - 1 else r["legs"].at[i, span]
        if i > 0:
            arrived[p].wait_recv()
        arrived[p] = send(src, dst, where)

    def legs_from(i):
        for p, (_, _, legs) in enumerate(pieces):
            if len(legs) > i:
                leg(p, i)

    for p in range(EARLY[k]):
        leg(p, 0)

    for copy in loads:
        copy.wait()
    r["ctx_t"][...] = r["ctx_v"][...].T

    def project(cols):
        params = bf16(f32(r["numer_v"][:, cols]) / weight)
        r["params"][:, cols] = params
        rows = jnp.dot(r["ctx_v"][...], params, preferred_element_type=jnp.float32)
        r["proj"][:, :, cols] = bf16(rows).reshape(tps, toks, WIDE)

    tiles(WIDE, project)
    w_copy = send(r["w_out"], r["w_in"], at((rep + (1 << k)) % reps, tp))

    far = (tp + tps // 2) % tps // 2 * 2
    up, down = ahead // 2 * 2, behind // 2 * 2
    e_up = send(r["proj"].at[far], r["part"].at[0], at(rep, ahead))
    e_down = send(r["proj"].at[far + 1], r["part"].at[1], at(rep, behind))
    a1.wait_recv()
    a2 = send(r["y_relay"].at[0], r["cots"].at[tp], at(over, flip))
    f_up = send(r["proj"].at[up + 1], r["sums"].at[1, 0], at(rep, ahead))
    f_down = send(r["proj"].at[down], r["sums"].at[0, 0], at(rep, behind))

    a2.wait_recv()
    c_up = send(r["cots"].at[flip], r["cots"].at[flip], at(rep, ahead))
    c_down = send(r["cots"].at[flip], r["cots"].at[flip], at(rep, behind))

    e_up.wait_recv()
    e_down.wait_recv()

    def join(cols):
        r["both"][0, :, cols] = bf16(f32(r["proj"][up, :, cols]) + f32(r["part"][0, :, cols]))
        r["both"][1, :, cols] = bf16(f32(r["proj"][down + 1, :, cols]) + f32(r["part"][1, :, cols]))

    tiles(FLAT, join)
    for copy in (b_up, b_down):
        copy.wait_recv()
    g_up = send(r["both"].at[0], r["sums"].at[0, 1], at(rep, ahead))
    g_down = send(r["both"].at[1], r["sums"].at[1, 1], at(rep, behind))

    c_up.wait_recv()
    c_down.wait_recv()
    d_up = send(r["cots"].at[down], r["cots"].at[down], at(rep, ahead))
    d_down = send(r["cots"].at[up + 1], r["cots"].at[up + 1], at(rep, behind))

    for copy in (f_up, f_down, g_up, g_down):
        copy.wait_recv()
    other = 1 - y_hi

    def total(cols):
        def of(half):
            mine = f32(r["proj"][x * 2 + half, :, cols])
            return mine + f32(r["sums"][half, 0, :, cols]) + f32(r["sums"][half, 1, :, cols])

        r["y_out"][:, cols] = bf16(of(other))
        r["own"][:, cols] = f32(r["res_v"][:, cols]) + of(y_hi)

    tiles(FLAT, total)
    legs_from(1)
    h1 = send(r["y_out"], r["y_relay"].at[1], at(over, tp))
    for p in range(EARLY[k], len(pieces)):
        leg(p, 0)

    d_up.wait_recv()
    d_down.wait_recv()
    h1.wait_recv()
    h2 = send(r["y_relay"].at[1], r["y_in"], at(over, flip))

    r["acc"][...] = jnp.zeros_like(r["acc"])

    def grads(cols):
        cot = r["cots"][:, :, cols].reshape(tps * toks, WIDE)
        slope = jnp.dot(r["ctx_t"][...], cot, preferred_element_type=jnp.float32)
        r["base"][:, cols] = 0.5 * f32(r["numer_v"][:, cols]) - LEARN * slope
        r["acc"][...] += lax.dot_general(
            cot, r["params"][:, cols], (((1,), (1,)), ((), ())), preferred_element_type=jnp.float32
        )

    tiles(WIDE, grads)
    r["ctx_v"][...] = bf16(r["acc"][...])
    stores = [local(r["ctx_v"], r["gctx"])]
    legs_from(2)

    h2.wait_recv()

    def finish(cols):
        r["res_v"][:, cols] = bf16(r["own"][:, cols] + f32(r["y_in"][:, cols]))

    tiles(FLAT, finish)
    stores.append(local(r["res_v"], r["out"]))
    w_copy.wait_recv()
    r["w_next"][0] = 0.5 * (weight + jnp.max(r["w_in"][...]))

    order = sorted(range(len(pieces)), key=lambda p: len(pieces[p][2]) > 1)
    for p in order:
        row, rows, _ = pieces[p]
        arrived[p].wait_recv()

        def mix(cols):
            value = r["base"][row : row + rows, cols] + 0.5 * f32(r["peer_v"][row : row + rows, cols])
            r["numer_v"][row : row + rows, cols] = bf16(value)

        tiles(FLAT, mix)
        stores.append(local(r["numer_v"].at[pl.ds(row, rows)], r["numer_next"].at[pl.ds(row, rows)]))

    for copy in stores:
        copy.wait()
    for copy in sends:
        copy.wait_send()


def step_at(k, reps, tps, context, residual, cotangent, numer, weight):
    toks, wide = residual.shape
    rows, feats = context.shape
    short, full = jnp.bfloat16, jnp.float32
    _, pieces = pieces_of(k)
    hops = sum(len(legs) for _, _, legs in pieces)
    n_legs = max(len(legs) for _, _, legs in pieces)
    leg_rows = sum(n for _, n, legs in pieces if len(legs) > 1)
    block = (toks, wide)
    hbm = pl.BlockSpec(memory_space=pl.ANY)
    smem = pl.BlockSpec(memory_space=pltpu.SMEM)
    scratch = {
        "numer_v": pltpu.VMEM((feats, wide), short),
        "params": pltpu.VMEM((feats, wide), short),
        "peer_v": pltpu.VMEM((feats, wide), short),
        "base": pltpu.VMEM((feats, wide), full),
        "legs": pltpu.VMEM((max(1, n_legs - 1), max(16, leg_rows), wide if leg_rows else 128), short),
        "ctx_v": pltpu.VMEM((rows, feats), short),
        "ctx_t": pltpu.VMEM((feats, rows), short),
        "acc": pltpu.VMEM((rows, feats), full),
        "cots": pltpu.VMEM((tps, *block), short),
        "proj": pltpu.VMEM((tps, *block), short),
        "part": pltpu.VMEM((2, *block), short),
        "both": pltpu.VMEM((2, *block), short),
        "sums": pltpu.VMEM((2, 2, *block), short),
        "y_relay": pltpu.VMEM((2, *block), short),
        "y_out": pltpu.VMEM(block, short),
        "y_in": pltpu.VMEM(block, short),
        "own": pltpu.VMEM(block, full),
        "res_v": pltpu.VMEM(block, short),
        "w_out": pltpu.VMEM((8, 128), full),
        "w_in": pltpu.VMEM((8, 128), full),
        "ss": pltpu.SemaphoreType.DMA((20 + hops,)),
        "rs": pltpu.SemaphoreType.DMA((20 + hops,)),
        "ls": pltpu.SemaphoreType.DMA((8 + len(pieces),)),
    }
    given = ("ctx", "res", "cot", "numer", "weight")
    made = ("out", "gctx", "numer_next", "w_next")
    return pl.pallas_call(
        functools.partial(kernel, k, reps, tps, (*given, *made, *scratch)),
        out_shape=(
            jax.ShapeDtypeStruct(residual.shape, short),
            jax.ShapeDtypeStruct(context.shape, short),
            jax.ShapeDtypeStruct(numer.shape, short),
            jax.ShapeDtypeStruct(weight.shape, full),
        ),
        in_specs=[hbm, hbm, hbm, hbm, smem],
        out_specs=(hbm, hbm, hbm, smem),
        scratch_shapes=list(scratch.values()),
        compiler_params=pltpu.CompilerParams(
            collective_id=k, has_side_effects=True, vmem_limit_bytes=63 * 2**20
        ),
        name=f"push_{k}",
    )(context, residual, cotangent, numer, weight)


def solution(mesh):
    reps, tps = mesh.shape["rep"], mesh.shape["tp"]
    both = P(("rep", "tp"), None)

    def on_device(context, residual, cotangent, numer, weight, step):
        k = jnp.remainder(step[0], jnp.int32(PEER_BITS + 1))
        branches = [functools.partial(step_at, bits, reps, tps) for bits in range(PEER_BITS + 1)]
        output, grad_ctx, numer_next, weight_next = lax.switch(
            k, branches, context, residual, cotangent, numer[0], weight
        )
        return output, grad_ctx, numer_next[None], weight_next

    return jax.shard_map(
        on_device,
        mesh=mesh,
        in_specs=(P("rep", "tp"), both, both, P("rep", "tp", None), P("rep"), P()),
        out_specs=(both, P("rep", "tp"), P("rep", "tp", None), P("rep")),
        check_vma=False,
    )
```

profile of v0, /device:TPU:72, one launch (start us, length us, event | category | flops | bytes accessed | tf_op | source)
XLA Modules:
  0.0 109.6 jit_solution(11224031518449823139)
XLA Ops:
  1.3 100.8 %conditional.1 = ((bf16[32,5120]{1,0:T(8,128)(2,1)S(1)}, bf16[256,384]{1,0:T(8,128)(2,1)S(1)}, bf16[384,5120]{1,0:T(8,128)(2,1)}, f32[1]{0:T(128)})) conditional(s32[]{:T(128)} %clamp.3, (bf16[256,384]{1,0:T(8,128)(2,1)}, bf16[32,5120]{1,0:T(8,128)(2,1)}, bf16[32,5120]{1,0:T(8,128)(2,1)}, ...), branch_computations={%region_0.1_spmd, %region_1.2_spmd, %region_2.3_spmd, %region_3.4_... | conditional | bytes 8 | solution.py:295
  1.3 100.7 %push_0.1 = (bf16[32,5120]{1,0:T(8,128)(2,1)S(1)}, bf16[256,384]{1,0:T(8,128)(2,1)S(1)}, bf16[384,5120]{1,0:T(8,128)(2,1)}, f32[1]{0:T(128)}) custom-call(bf16[256,384]{1,0:T(8,128)(2,1)} %get-tuple-element.62.refs_0_, bf16[32,5120]{1,0:T(8,128)(2,1)} %get-tuple-element.63.refs_1_, bf16[32,5120]{1,0:T(8,128)(2,1)} %get-tuple-element.64.refs_2_, ...), custom_call_target="tpu_custom_call" | custom-call | tf_op jit(solution)/shard_map/cond/branch_0_fun/push_0/pallas_call | solution.py:270
  102.1 0.7 copy.31
  102.8 0.7 copy.32
  103.5 4.3 %copy.33 = bf16[1,384,5120]{2,1,0:T(8,128)(2,1)} copy(bf16[1,384,5120]{2,1,0:T(8,128)(2,1)} %bitcast.10) | data formatting | bytes 7864320
where the time goes:
time: 110 us
  Pallas kernels  101 us (92%)
  local copies, waits for them, and re-layouts  5.69 us (5%)
  between operations  3.11 us (3%)
    pallas_call x1, Pallas kernels, step_at(): pl.pallas_call(functools.partial(kernel, k, reps, tps, (*given, *made, *s...  101 us
    unnamed x3, local copies, waits for them, and re-layouts  5.69 us

commit v1 on v0

--- a/solution.py
+++ b/solution.py
@@ -11,22 +11,49 @@
 LEARN = 0.001
 MESH = pl.DeviceIdType.MESH
 WIDE = 256
-FLAT = 1024
+FLAT = 512
 
 PLANS = (
-    (((1,), 32, 12),),
-    (((2,), 32, 12),),
-    (((-12, -12, -4), 16, 2), ((4,), 32, 11)),
-    (((-12, -12), 16, 6), ((8,), 32, 9)),
+    (((1,), (256, 64, 32, 32)),),
+    (((2,), (192, 64, 64, 32, 32)),),
+    (((-12, -12, -4), (16,) * 2), ((4,), (32,) * 11)),
+    (((-12, -12), (16,) * 6), ((8,), (32,) * 9)),
 )
-EARLY = (5, 5, 13, 15)
+WINDOW = 3
+
+
+def legs(leg, *pieces):
+    return tuple((p, leg) for p in pieces)
+
+
+STARTS = (
+    {"entry": legs(0, 0), "total": legs(0, 1), "relay": legs(0, 2, 3)},
+    {"entry": legs(0, 0), "relay": legs(0, 1), "grads": legs(0, 2)},
+    {
+        "entry": legs(0, 0, 1, 2, 3, 4),
+        "project": legs(0, 5),
+        "join": legs(0, 6),
+        "total": legs(1, 0, 1) + legs(0, 7),
+        "relay": legs(0, 8, 9),
+        "grads": legs(0, 10),
+        "mix": legs(2, 0, 1),
+    },
+    {
+        "entry": legs(0, 0, 1, 2, 6, 7, 8),
+        "join": legs(0, 3, 4, 5),
+        "total": legs(0, 9),
+        "relay": legs(0, 10),
+        "grads": legs(1, 0, 1, 2) + legs(0, 11),
+        "mix4": legs(1, 3, 4, 5),
+    },
+)
 
 
 def pieces_of(k):
     row, pieces = 0, []
-    for legs, rows, count in PLANS[k]:
-        for _ in range(count):
-            pieces.append((row, rows, legs))
+    for offsets, sizes in PLANS[k]:
+        for rows in sizes:
+            pieces.append((row, rows, offsets))
             row += rows
     return row, pieces
 
@@ -68,12 +95,13 @@
         copy.start()
         return copy
 
-    def tiles(n, body):
+    def tiles(n, body, part=0, parts=1):
         def step(j, carry):
             body(pl.ds(pl.multiple_of(j * n, n), n))
             return carry
 
-        lax.fori_loop(0, wide // n, step, 0)
+        count = wide // n // parts
+        lax.fori_loop(part * count, (part + 1) * count, step, 0)
 
     f32 = lambda a: a.astype(jnp.float32)
     bf16 = lambda a: a.astype(jnp.bfloat16)
@@ -87,7 +115,7 @@
     weight = r["weight"][0]
     r["w_out"][...] = jnp.full(r["w_out"].shape, weight, jnp.float32)
 
-    hops = sorted({hop for _, _, legs in pieces for hop in legs} | {1 << k})
+    hops = sorted({hop for _, _, offsets in pieces for hop in offsets} | {1 << k})
     near = [at(over, tp), at(over, flip), at(rep, ahead), at(rep, behind)]
     near += [at((rep + sign * hop) % reps, tp) for hop in hops for sign in (1, -1)]
     barrier = pltpu.get_barrier_semaphore()
@@ -95,29 +123,28 @@
         pl.semaphore_signal(barrier, inc=1, device_id=where, device_id_type=MESH)
     pl.semaphore_wait(barrier, len(near))
 
-    a1 = send(r["cot"], r["y_relay"].at[0], at(over, tp))
+    halves = [pl.ds(i * toks // 2, toks // 2) for i in range(2)]
+    a1 = [send(r["cot"].at[half], r["y_relay"].at[0, half], at(over, tp)) for half in halves]
     b_up = send(r["cot"], r["cots"].at[tp], at(rep, ahead))
     b_down = send(r["cot"], r["cots"].at[tp], at(rep, behind))
 
     arrived = {}
 
     def leg(p, i):
-        row, rows, legs = pieces[p]
-        where = at((rep + legs[i]) % reps, tp)
+        row, rows, offsets = pieces[p]
+        where = at((rep + offsets[i]) % reps, tp)
         span = pl.ds(row, rows)
         src = r["numer"].at[span] if i == 0 else r["legs"].at[i - 1, span]
-        dst = r["peer_v"].at[span] if i == len(legs) - 1 else r["legs"].at[i, span]
+        dst = r["peer_v"].at[span] if i == len(offsets) - 1 else r["legs"].at[i, span]
         if i > 0:
             arrived[p].wait_recv()
         arrived[p] = send(src, dst, where)
 
-    def legs_from(i):
-        for p, (_, _, legs) in enumerate(pieces):
-            if len(legs) > i:
-                leg(p, i)
-
-    for p in range(EARLY[k]):
-        leg(p, 0)
+    def start_at(point):
+        for p, i in STARTS[k].get(point, ()):
+            leg(p, i)
+
+    start_at("entry")
 
     for copy in loads:
         copy.wait()
@@ -129,42 +156,40 @@
         rows = jnp.dot(r["ctx_v"][...], params, preferred_element_type=jnp.float32)
         r["proj"][:, :, cols] = bf16(rows).reshape(tps, toks, WIDE)
 
-    tiles(WIDE, project)
-    w_copy = send(r["w_out"], r["w_in"], at((rep + (1 << k)) % reps, tp))
-
     far = (tp + tps // 2) % tps // 2 * 2
     up, down = ahead // 2 * 2, behind // 2 * 2
-    e_up = send(r["proj"].at[far], r["part"].at[0], at(rep, ahead))
-    e_down = send(r["proj"].at[far + 1], r["part"].at[1], at(rep, behind))
-    a1.wait_recv()
-    a2 = send(r["y_relay"].at[0], r["cots"].at[tp], at(over, flip))
-    f_up = send(r["proj"].at[up + 1], r["sums"].at[1, 0], at(rep, ahead))
-    f_down = send(r["proj"].at[down], r["sums"].at[0, 0], at(rep, behind))
-
-    a2.wait_recv()
-    c_up = send(r["cots"].at[flip], r["cots"].at[flip], at(rep, ahead))
-    c_down = send(r["cots"].at[flip], r["cots"].at[flip], at(rep, behind))
-
-    e_up.wait_recv()
-    e_down.wait_recv()
+    parts = [pl.ds(i * wide // 2, wide // 2) for i in range(2)]
+
+    e_up, e_down, g_up, g_down = [], [], [], []
+    for i, part in enumerate(parts):
+        tiles(WIDE, project, i, 2)
+        e_up.append(send(r["proj"].at[far, :, part], r["part"].at[0, :, part], at(rep, ahead)))
+        e_down.append(send(r["proj"].at[far + 1, :, part], r["part"].at[1, :, part], at(rep, behind)))
+    w_copy = send(r["w_out"], r["w_in"], at((rep + (1 << k)) % reps, tp))
+    start_at("project")
+    a2 = []
+    for copy, half in zip(a1, halves):
+        copy.wait_recv()
+        a2.append(send(r["y_relay"].at[0, half], r["cots"].at[tp, half], at(over, flip)))
 
     def join(cols):
         r["both"][0, :, cols] = bf16(f32(r["proj"][up, :, cols]) + f32(r["part"][0, :, cols]))
         r["both"][1, :, cols] = bf16(f32(r["proj"][down + 1, :, cols]) + f32(r["part"][1, :, cols]))
 
-    tiles(FLAT, join)
-    for copy in (b_up, b_down):
-        copy.wait_recv()
-    g_up = send(r["both"].at[0], r["sums"].at[0, 1], at(rep, ahead))
-    g_down = send(r["both"].at[1], r["sums"].at[1, 1], at(rep, behind))
-
-    c_up.wait_recv()
-    c_down.wait_recv()
-    d_up = send(r["cots"].at[down], r["cots"].at[down], at(rep, ahead))
-    d_down = send(r["cots"].at[up + 1], r["cots"].at[up + 1], at(rep, behind))
-
-    for copy in (f_up, f_down, g_up, g_down):
-        copy.wait_recv()
+    for i, part in enumerate(parts):
+        e_up[i].wait_recv()
+        e_down[i].wait_recv()
+        tiles(FLAT, join, i, 2)
+        g_up.append(send(r["both"].at[0, :, part], r["sums"].at[0, 1, :, part], at(rep, ahead)))
+        g_down.append(send(r["both"].at[1, :, part], r["sums"].at[1, 1, :, part], at(rep, behind)))
+    f_up = send(r["proj"].at[up + 1], r["sums"].at[1, 0], at(rep, ahead))
+    f_down = send(r["proj"].at[down], r["sums"].at[0, 0], at(rep, behind))
+    start_at("join")
+
+    for copy in (*g_up, *g_down, f_up, f_down, *a2):
+        copy.wait_recv()
+    c_up = send(r["cots"].at[flip], r["cots"].at[flip], at(rep, ahead))
+    c_down = send(r["cots"].at[flip], r["cots"].at[flip], at(rep, behind))
     other = 1 - y_hi
 
     def total(cols):
@@ -176,15 +201,21 @@
         r["own"][:, cols] = f32(r["res_v"][:, cols]) + of(y_hi)
 
     tiles(FLAT, total)
-    legs_from(1)
-    h1 = send(r["y_out"], r["y_relay"].at[1], at(over, tp))
-    for p in range(EARLY[k], len(pieces)):
-        leg(p, 0)
-
+    h1 = [send(r["y_out"].at[half], r["y_relay"].at[1, half], at(over, tp)) for half in halves]
+    start_at("total")
+
+    for copy in (b_up, b_down, c_up, c_down):
+        copy.wait_recv()
+    d_up = send(r["cots"].at[down], r["cots"].at[down], at(rep, ahead))
+    d_down = send(r["cots"].at[up + 1], r["cots"].at[up + 1], at(rep, behind))
+    h2 = []
+    for copy, half in zip(h1, halves):
+        copy.wait_recv()
+        h2.append(send(r["y_relay"].at[1, half], r["y_in"].at[half], at(over, flip)))
+    start_at("relay")
     d_up.wait_recv()
     d_down.wait_recv()
-    h1.wait_recv()
-    h2 = send(r["y_relay"].at[1], r["y_in"], at(over, flip))
+    start_at("grads")
 
     r["acc"][...] = jnp.zeros_like(r["acc"])
 
@@ -197,34 +228,35 @@
         )
 
     tiles(WIDE, grads)
-    r["ctx_v"][...] = bf16(r["acc"][...])
-    stores = [local(r["ctx_v"], r["gctx"])]
-    legs_from(2)
-
-    h2.wait_recv()
+    r["gctx"][...] = bf16(r["acc"][...])
+
+    for copy in h2:
+        copy.wait_recv()
 
     def finish(cols):
-        r["res_v"][:, cols] = bf16(r["own"][:, cols] + f32(r["y_in"][:, cols]))
+        r["out"][:, cols] = bf16(r["own"][:, cols] + f32(r["y_in"][:, cols]))
 
     tiles(FLAT, finish)
-    stores.append(local(r["res_v"], r["out"]))
     w_copy.wait_recv()
     r["w_next"][0] = 0.5 * (weight + jnp.max(r["w_in"][...]))
 
-    order = sorted(range(len(pieces)), key=lambda p: len(pieces[p][2]) > 1)
-    for p in order:
+    start_at("mix")
+    direct = [p for p in range(len(pieces)) if len(pieces[p][2]) == 1]
+    relayed = [p for p in range(len(pieces)) if len(pieces[p][2]) > 1]
+    for n, p in enumerate(direct + relayed):
         row, rows, _ = pieces[p]
+        start_at(f"mix{n}")
         arrived[p].wait_recv()
+        for later in direct[: n + WINDOW + 1]:
+            if later not in arrived:
+                leg(later, 0)
 
         def mix(cols):
             value = r["base"][row : row + rows, cols] + 0.5 * f32(r["peer_v"][row : row + rows, cols])
-            r["numer_v"][row : row + rows, cols] = bf16(value)
+            r["numer_next"][row : row + rows, cols] = bf16(value)
 
         tiles(FLAT, mix)
-        stores.append(local(r["numer_v"].at[pl.ds(row, rows)], r["numer_next"].at[pl.ds(row, rows)]))
-
-    for copy in stores:
-        copy.wait()
+
     for copy in sends:
         copy.wait_send()
 
@@ -234,12 +266,13 @@
     rows, feats = context.shape
     short, full = jnp.bfloat16, jnp.float32
     _, pieces = pieces_of(k)
-    hops = sum(len(legs) for _, _, legs in pieces)
-    n_legs = max(len(legs) for _, _, legs in pieces)
-    leg_rows = sum(n for _, n, legs in pieces if len(legs) > 1)
+    hops = sum(len(offsets) for _, _, offsets in pieces)
+    n_legs = max(len(offsets) for _, _, offsets in pieces)
+    leg_rows = sum(n for _, n, offsets in pieces if len(offsets) > 1)
     block = (toks, wide)
     hbm = pl.BlockSpec(memory_space=pl.ANY)
     smem = pl.BlockSpec(memory_space=pltpu.SMEM)
+    vmem = pl.BlockSpec(memory_space=pltpu.VMEM)
     scratch = {
         "numer_v": pltpu.VMEM((feats, wide), short),
         "params": pltpu.VMEM((feats, wide), short),
@@ -261,9 +294,9 @@
         "res_v": pltpu.VMEM(block, short),
         "w_out": pltpu.VMEM((8, 128), full),
         "w_in": pltpu.VMEM((8, 128), full),
-        "ss": pltpu.SemaphoreType.DMA((20 + hops,)),
-        "rs": pltpu.SemaphoreType.DMA((20 + hops,)),
-        "ls": pltpu.SemaphoreType.DMA((8 + len(pieces),)),
+        "ss": pltpu.SemaphoreType.DMA((26 + hops,)),
+        "rs": pltpu.SemaphoreType.DMA((26 + hops,)),
+        "ls": pltpu.SemaphoreType.DMA((4,)),
     }
     given = ("ctx", "res", "cot", "numer", "weight")
     made = ("out", "gctx", "numer_next", "w_next")
@@ -276,10 +309,10 @@
             jax.ShapeDtypeStruct(weight.shape, full),
         ),
         in_specs=[hbm, hbm, hbm, hbm, smem],
-        out_specs=(hbm, hbm, hbm, smem),
+        out_specs=(vmem, vmem, vmem, smem),
         scratch_shapes=list(scratch.values()),
         compiler_params=pltpu.CompilerParams(
-            collective_id=k, has_side_effects=True, vmem_limit_bytes=63 * 2**20
+            collective_id=k, has_side_effects=True, vmem_limit_bytes=48 * 2**20
         ),
         name=f"push_{k}",
     )(context, residual, cotangent, numer, weight)

time: 110 us -> 95.8 us (0.87)
  the two profiles are of different devices: /device:TPU:72 before, /device:TPU:2 now
where the time goes in v1:
time: 95.8 us; the launch traced here: 95.7 us
  Pallas kernels  89.3 us (93%)
  local copies, waits for them, and re-layouts  3.33 us (3%)
  between operations  2.99 us (3%)
    pallas_call x1, Pallas kernels, step_at(): pl.pallas_call(functools.partial(kernel, k, reps, tps, (*given, *made, *s...  89.3 us
    unnamed x3, local copies, waits for them, and re-layouts  3.33 us

profile of v1, /device:TPU:2, one launch (start us, length us, event | category | flops | bytes accessed | tf_op | source)
XLA Modules:
  0.0 95.7 jit_solution(7560518740953193063)
XLA Ops:
  1.3 89.4 %conditional.1 = ((bf16[32,5120]{1,0:T(8,128)(2,1)S(1)}, bf16[256,384]{1,0:T(8,128)(2,1)S(1)}, bf16[384,5120]{1,0:T(8,128)(2,1)S(1)}, f32[1]{0:T(128)})) conditional(s32[]{:T(128)} %clamp.3, (bf16[256,384]{1,0:T(8,128)(2,1)}, bf16[32,5120]{1,0:T(8,128)(2,1)}, bf16[32,5120]{1,0:T(8,128)(2,1)}, ...), branch_computations={%region_0.1_spmd, %region_1.2_spmd, %region_2.3_spmd, %region_3.4_... | conditional | bytes 8 | solution.py:328
  1.3 89.3 %push_2.1 = (bf16[32,5120]{1,0:T(8,128)(2,1)S(1)}, bf16[256,384]{1,0:T(8,128)(2,1)S(1)}, bf16[384,5120]{1,0:T(8,128)(2,1)S(1)}, f32[1]{0:T(128)}) custom-call(bf16[256,384]{1,0:T(8,128)(2,1)} %get-tuple-element.72.refs_0_, bf16[32,5120]{1,0:T(8,128)(2,1)} %get-tuple-element.73.refs_1_, bf16[32,5120]{1,0:T(8,128)(2,1)} %get-tuple-element.74.refs_2_, ...), custom_call_target="tpu_custom_call" | custom-call | tf_op jit(solution)/shard_map/cond/branch_2_fun/push_2/pallas_call | solution.py:303
  90.7 0.7 copy.31
  91.4 0.7 copy.32
  92.1 1.9 %copy.33 = bf16[1,384,5120]{2,1,0:T(8,128)(2,1)} copy(bf16[1,384,5120]{2,1,0:T(8,128)(2,1)S(1)} %bitcast.10) | data formatting | bytes 7864320

commit v2 on v1

--- a/solution.py
+++ b/solution.py
@@ -13,11 +13,12 @@
 WIDE = 256
 FLAT = 512
 
+GROUP = 4
 PLANS = (
-    (((1,), (256, 64, 32, 32)),),
-    (((2,), (192, 64, 64, 32, 32)),),
-    (((-12, -12, -4), (16,) * 2), ((4,), (32,) * 11)),
-    (((-12, -12), (16,) * 6), ((8,), (32,) * 9)),
+    (((1, GROUP), (96, 96, 64)), ((1,), (64, 48, 16))),
+    (((2, GROUP), (64, 64)), ((2,), (64, 64, 48, 32, 32, 16))),
+    (((-12, -12, -4), (16,) * 2), ((4,), (32,) * 10 + (16,) * 2)),
+    (((-12, -12), (16,) * 6), ((8,), (32,) * 8 + (16,) * 2)),
 )
 WINDOW = 3
 
@@ -27,23 +28,31 @@
 
 
 STARTS = (
-    {"entry": legs(0, 0), "total": legs(0, 1), "relay": legs(0, 2, 3)},
-    {"entry": legs(0, 0), "relay": legs(0, 1), "grads": legs(0, 2)},
     {
-        "entry": legs(0, 0, 1, 2, 3, 4),
-        "project": legs(0, 5),
-        "join": legs(0, 6),
-        "total": legs(1, 0, 1) + legs(0, 7),
-        "relay": legs(0, 8, 9),
-        "grads": legs(0, 10),
+        "entry": legs(0, 0, 1, 2),
+        "join": legs(1, 0),
+        "total": legs(0, 3, 4, 5) + legs(1, 1, 2),
+    },
+    {
+        "entry": legs(0, 0, 1),
+        "join": legs(1, 0),
+        "total": legs(0, 2, 3, 4, 5, 6, 7) + legs(1, 1),
+    },
+    {
+        "entry": legs(0, 0, 1, 2, 3, 4, 5),
+        "project": legs(0, 6),
+        "join": legs(0, 7),
+        "total": legs(1, 0, 1) + legs(0, 8),
+        "relay": legs(0, 9, 10),
+        "grads": legs(0, 11),
         "mix": legs(2, 0, 1),
     },
     {
-        "entry": legs(0, 0, 1, 2, 6, 7, 8),
+        "entry": legs(0, 0, 1, 2, 6, 7, 8, 9),
         "join": legs(0, 3, 4, 5),
-        "total": legs(0, 9),
-        "relay": legs(0, 10),
-        "grads": legs(1, 0, 1, 2) + legs(0, 11),
+        "total": legs(0, 10),
+        "relay": legs(0, 11),
+        "grads": legs(1, 0, 1, 2) + legs(0, 12),
         "mix4": legs(1, 3, 4, 5),
     },
 )
@@ -73,10 +82,10 @@
     used = {"s": 0, "r": 0}
     sends = []
 
-    def send(src, dst, where):
+    def remote(src, dst, where):
         i = used["s"]
         used["s"] += 1
-        copy = pltpu.make_async_remote_copy(
+        return pltpu.make_async_remote_copy(
             src_ref=src,
             dst_ref=dst,
             send_sem=r["ss"].at[i],
@@ -84,6 +93,9 @@
             device_id=where,
             device_id_type=MESH,
         )
+
+    def send(src, dst, where):
+        copy = remote(src, dst, where)
         copy.start()
         sends.append(copy)
         return copy
@@ -118,6 +130,13 @@
     hops = sorted({hop for _, _, offsets in pieces for hop in offsets} | {1 << k})
     near = [at(over, tp), at(over, flip), at(rep, ahead), at(rep, behind)]
     near += [at((rep + sign * hop) % reps, tp) for hop in hops for sign in (1, -1)]
+    grouped = 1 << k < GROUP
+    place = rep % GROUP
+    beside = rep - place + (place + (1 << k)) % GROUP
+    passes = place < 1 << k
+    if grouped:
+        near += [at(beside, tp), at(rep - place + (place + GROUP - (1 << k)) % GROUP, tp)]
+        near += [at((rep + sign * GROUP) % reps, tp) for sign in (1, -1)]
     barrier = pltpu.get_barrier_semaphore()
     for where in near:
         pl.semaphore_signal(barrier, inc=1, device_id=where, device_id_type=MESH)
@@ -128,14 +147,27 @@
     b_up = send(r["cot"], r["cots"].at[tp], at(rep, ahead))
     b_down = send(r["cot"], r["cots"].at[tp], at(rep, behind))
 
-    arrived = {}
+    arrived, passed = {}, {}
+
+    def pass_on(p):
+        row, rows, _ = pieces[p]
+        span = pl.ds(row, rows)
+        passed[p] = remote(r["peer_v"].at[0, span], r["peer_v"].at[1, span], at((rep + GROUP) % reps, tp))
+
+        @pl.when(passes)
+        def _():
+            arrived[p].wait_recv()
+            passed[p].start()
 
     def leg(p, i):
         row, rows, offsets = pieces[p]
-        where = at((rep + offsets[i]) % reps, tp)
+        if grouped and i > 0:
+            pass_on(p)
+            return
+        where = at(beside if grouped and len(offsets) > 1 else (rep + offsets[i]) % reps, tp)
         span = pl.ds(row, rows)
         src = r["numer"].at[span] if i == 0 else r["legs"].at[i - 1, span]
-        dst = r["peer_v"].at[span] if i == len(offsets) - 1 else r["legs"].at[i, span]
+        dst = r["peer_v"].at[0, span] if grouped or i == len(offsets) - 1 else r["legs"].at[i, span]
         if i > 0:
             arrived[p].wait_recv()
         arrived[p] = send(src, dst, where)
@@ -243,22 +275,33 @@
     start_at("mix")
     direct = [p for p in range(len(pieces)) if len(pieces[p][2]) == 1]
     relayed = [p for p in range(len(pieces)) if len(pieces[p][2]) > 1]
-    for n, p in enumerate(direct + relayed):
+    def mix_piece(p):
         row, rows, _ = pieces[p]
+        half = 0
+        if p in passed:
+            half = jnp.where(passes, 1, 0)
+            pl.when(passes)(passed[p].wait_recv)
+            pl.when(jnp.logical_not(passes))(arrived[p].wait_recv)
+        else:
+            arrived[p].wait_recv()
+
+        def mix(cols):
+            value = r["base"][row : row + rows, cols] + 0.5 * f32(r["peer_v"][half, row : row + rows, cols])
+            r["numer_next"][row : row + rows, cols] = bf16(value)
+
+        tiles(FLAT, mix)
+
+    for n, p in enumerate(range(len(pieces)) if grouped else direct + relayed):
         start_at(f"mix{n}")
-        arrived[p].wait_recv()
+        mix_piece(p)
         for later in direct[: n + WINDOW + 1]:
             if later not in arrived:
                 leg(later, 0)
 
-        def mix(cols):
-            value = r["base"][row : row + rows, cols] + 0.5 * f32(r["peer_v"][row : row + rows, cols])
-            r["numer_next"][row : row + rows, cols] = bf16(value)
-
-        tiles(FLAT, mix)
-
     for copy in sends:
         copy.wait_send()
+    for copy in passed.values():
+        pl.when(passes)(copy.wait_send)
 
 
 def step_at(k, reps, tps, context, residual, cotangent, numer, weight):
@@ -268,7 +311,7 @@
     _, pieces = pieces_of(k)
     hops = sum(len(offsets) for _, _, offsets in pieces)
     n_legs = max(len(offsets) for _, _, offsets in pieces)
-    leg_rows = sum(n for _, n, offsets in pieces if len(offsets) > 1)
+    leg_rows = 0 if 1 << k < GROUP else sum(n for _, n, offsets in pieces if len(offsets) > 1)
     block = (toks, wide)
     hbm = pl.BlockSpec(memory_space=pl.ANY)
     smem = pl.BlockSpec(memory_space=pltpu.SMEM)
@@ -276,7 +319,7 @@
     scratch = {
         "numer_v": pltpu.VMEM((feats, wide), short),
         "params": pltpu.VMEM((feats, wide), short),
-        "peer_v": pltpu.VMEM((feats, wide), short),
+        "peer_v": pltpu.VMEM((2 if 1 << k < GROUP else 1, feats, wide), short),
         "base": pltpu.VMEM((feats, wide), full),
         "legs": pltpu.VMEM((max(1, n_legs - 1), max(16, leg_rows), wide if leg_rows else 128), short),
         "ctx_v": pltpu.VMEM((rows, feats), short),
@@ -294,8 +337,8 @@
         "res_v": pltpu.VMEM(block, short),
         "w_out": pltpu.VMEM((8, 128), full),
         "w_in": pltpu.VMEM((8, 128), full),
-        "ss": pltpu.SemaphoreType.DMA((26 + hops,)),
-        "rs": pltpu.SemaphoreType.DMA((26 + hops,)),
+        "ss": pltpu.SemaphoreType.DMA((26 + hops + len(pieces),)),
+        "rs": pltpu.SemaphoreType.DMA((26 + hops + len(pieces),)),
         "ls": pltpu.SemaphoreType.DMA((4,)),
     }
     given = ("ctx", "res", "cot", "numer", "weight")

time: 95.8 us -> 147 us (1.53); the launches traced: 95.7 us -> 145 us
  Pallas kernels: 89.3 us -> 139 us
    pallas_call x1, Pallas kernels: 89.3 us -> 139 us  [step_at(): pl.pallas_call(functools.partial(kernel, k, reps, tps, (*given, *made, *s...]
where the time goes in v2:
time: 147 us; the launch traced here: 145 us
  Pallas kernels  139 us (95%)
  local copies, waits for them, and re-layouts  3.33 us (2%)
  between operations  2.99 us (2%)
    pallas_call x1, Pallas kernels, step_at(): pl.pallas_call(functools.partial(kernel, k, reps, tps, (*given, *made, *s...  139 us
    unnamed x3, local copies, waits for them, and re-layouts  3.33 us

profile of v2, /device:TPU:2, one launch (start us, length us, event | category | flops | bytes accessed | tf_op | source)
XLA Modules:
  0.0 145.3 jit_solution(15110250792078494830)
XLA Ops:
  1.3 139.0 %conditional.1 = ((bf16[32,5120]{1,0:T(8,128)(2,1)S(1)}, bf16[256,384]{1,0:T(8,128)(2,1)S(1)}, bf16[384,5120]{1,0:T(8,128)(2,1)S(1)}, f32[1]{0:T(128)})) conditional(s32[]{:T(128)} %clamp.3, (bf16[256,384]{1,0:T(8,128)(2,1)}, bf16[32,5120]{1,0:T(8,128)(2,1)}, bf16[32,5120]{1,0:T(8,128)(2,1)}, ...), branch_computations={%region_0.1_spmd, %region_1.2_spmd, %region_2.3_spmd, %region_3.4_... | conditional | bytes 8 | solution.py:371
  1.3 139.0 %push_3.1 = (bf16[32,5120]{1,0:T(8,128)(2,1)S(1)}, bf16[256,384]{1,0:T(8,128)(2,1)S(1)}, bf16[384,5120]{1,0:T(8,128)(2,1)S(1)}, f32[1]{0:T(128)}) custom-call(bf16[256,384]{1,0:T(8,128)(2,1)} %get-tuple-element.77.refs_0_, bf16[32,5120]{1,0:T(8,128)(2,1)} %get-tuple-element.78.refs_1_, bf16[32,5120]{1,0:T(8,128)(2,1)} %get-tuple-element.79.refs_2_, ...), custom_call_target="tpu_custom_call" | custom-call | tf_op jit(solution)/shard_map/cond/branch_3_fun/push_3/pallas_call | solution.py:346
  140.3 0.7 copy.31
  141.0 0.7 copy.32
  141.7 1.9 %copy.33 = bf16[1,384,5120]{2,1,0:T(8,128)(2,1)} copy(bf16[1,384,5120]{2,1,0:T(8,128)(2,1)S(1)} %bitcast.10) | data formatting | bytes 7864320
